TPU v7x, 32 devices: a whole 2x2x4 slice. The times are simulated.
32 devices in a mesh: dp: 8 (over z, y), tensor: 4 (over x, core).
Axes of the slice: x: 2, y: 2, z: 4, core: 2. Of those that a mesh axis runs over, the one named last changes fastest.
Arguments:
- gradients: bfloat16 [8, 2, 256, 1792], P('dp', None, None, 'tensor'), may hold values from -16 to 16, as said below
- errors: float32 [8, 2, 256, 1792], P('dp', None, None, 'tensor'), may hold values from -4 to 4
- start_factors: float32 [2, 1792, 32], P(None, 'tensor'), may hold values from -5 to 5
- moments: float32 [2, 256, 1792], P(None, 'dp', 'tensor'), may hold values from -2 to 2
- weights: float32 [2, 256, 1792], P(None, 'dp', 'tensor'), may hold values from -5 to 5
- vector_grads: bfloat16 [8, 5, 1792], P('dp', None, 'tensor'), may hold values from -16 to 16, as said below
- vector_moments: float32 [5, 1792], P(None, 'tensor'), may hold values from -2 to 2
- vector_weights: float32 [5, 1792], P(None, 'tensor'), may hold values from 0.5 to 1.5
Outputs:
- new_errors: float32 [8, 2, 256, 1792], P('dp', None, None, 'tensor')
- new_moments: float32 [2, 256, 1792], P(None, 'dp', 'tensor')
- new_weights: bfloat16 [2, 256, 1792], P(None, None, 'tensor')
- new_vector_moments: float32 [5, 1792], P(None, 'tensor')
- new_vector_weights: float32 [5, 1792], P(None, 'tensor')
Inputs may be any that keep to these rules, and one draw needn't show every extreme that they name: `gradients`: each replica's gradient is a part common to all replicas plus its own part. `vector_grads`: each replica's gradient is a part common to all replicas plus its own part.
All inputs are finite; a program needn't handle non-finite values.
Results may differ from a plain program's by a relative error of at most 0.0004.
Values may be sent and summed in bfloat16 or wider, within the bound.
A program may use at most 64 MiB of HBM per device.

v0:
```python
import jax
import jax.numpy as jnp
from jax import lax
from jax.sharding import PartitionSpec as P

ROUNDS = 2
momentum_coef = 0.9
step_rate = 0.1


def basis_from(gram_mat, summed):
    factor_low = jnp.linalg.cholesky(gram_mat)
    return lax.linalg.triangular_solve(
        factor_low, summed, left_side=False, lower=True, transpose_a=True
    )


def left_basis(mixed, right_f):
    partial_value = jnp.einsum("mkd,mdr->mkr", mixed, right_f, precision=lax.Precision.HIGHEST)
    summed = lax.psum(partial_value, ("dp", "tensor"))
    gram_mat = jnp.einsum("mkr,mks->mrs", summed, summed, precision=lax.Precision.HIGHEST)
    return basis_from(gram_mat, summed)


def update(mixed, start, moments, weights):
    right_f = start
    for round_idx in range(ROUNDS):
        basis_now = left_basis(mixed, right_f)
        right_part = jnp.einsum("mkd,mkr->mdr", mixed, basis_now, precision=lax.Precision.HIGHEST)
        right_f = lax.psum(right_part, "dp")
    replicas = lax.axis_size("dp")
    approx = (
        jnp.einsum("mkr,mdr->mkd", basis_now, right_f, precision=lax.Precision.HIGHEST) / replicas
    )
    fresh_errors = mixed - approx
    own_rows = moments.shape[1]
    my_rows = lax.dynamic_slice_in_dim(approx, lax.axis_index("dp") * own_rows, own_rows, 1)
    fresh_moments = momentum_coef * moments + my_rows
    fresh_weights = (weights - step_rate * fresh_moments).astype(jnp.bfloat16)
    regathered = lax.all_gather(fresh_weights, "dp", axis=1, tiled=True)
    return (fresh_errors, fresh_moments, regathered)


def per_device(
    gradients, errors, start_factors, moments, weights, vector_grads, vector_moments, vector_weights
):
    mixed = gradients[0].astype(jnp.float32) + errors[0]
    fresh_errors, fresh_moments, regathered = update(mixed, start_factors, moments, weights)
    vector_total = lax.psum(vector_grads[0].astype(jnp.float32), "dp")
    vector_mean = vector_total / lax.axis_size("dp")
    fresh_vector_moments = momentum_coef * vector_moments + vector_mean
    fresh_vector_weights = vector_weights - step_rate * fresh_vector_moments
    return (
        fresh_errors[None],
        fresh_moments,
        regathered,
        fresh_vector_moments,
        fresh_vector_weights,
    )


def solution(mesh):
    in_specs = (
        P("dp", None, None, "tensor"),
        P("dp", None, None, "tensor"),
        P(None, "tensor", None),
        P(None, "dp", "tensor"),
        P(None, "dp", "tensor"),
        P("dp", None, "tensor"),
        P(None, "tensor"),
        P(None, "tensor"),
    )
    out_specs = (
        P("dp", None, None, "tensor"),
        P(None, "dp", "tensor"),
        P(None, None, "tensor"),
        P(None, "tensor"),
        P(None, "tensor"),
    )
    return jax.shard_map(
        per_device, mesh=mesh, in_specs=in_specs, out_specs=out_specs, check_vma=False
    )
```

profile of v0, /device:TPU:0, one launch (start us, length us, event | category | flops | bytes accessed | tf_op | source)
XLA Modules:
  0.0 471.9 jit_solution(15930844537223940268)
XLA Ops:
  7.2 0.8 copy-done
  8.1 2.6 fusion.6
  10.8 123.7 %all-reduce.5.cloned.1.call-done = f32[2,256,32]{1,2,0:T(8,128)} async-done(((f32[2,256,32]{1,2,0:T(8,128)}), f32[2,256,32]{1,2,0:T(8,128)}) %all-reduce.5.cloned.1.call-update) | async-done | bytes 65552 | tf_op jit(solution)/shard_map/psum | solution.py:20
  134.5 1.1 fusion.13
  135.7 5.9 %custom-call.8 = f32[2,32,32]{2,1,0:T(8,128)S(1)} custom-call(f32[2,32,32]{2,1,0:T(8,128)S(1)} %fusion.12), custom_call_target="Cholesky" | custom-call | tf_op jit(solution)/shard_map/jit(cholesky)/cholesky | solution.py:12
  141.6 0.1 compare_reduce_fusion.1
  141.8 4.9 %custom-call.9 = f32[2,1,32,32]{2,3,1,0:T(8,128)S(1)} custom-call(f32[2,1,32,32]{3,2,1,0:T(8,128)S(1)} %select_bitcast_fusion.1), custom_call_target="InvertDiagBlocksLowerTriangular" | custom-call | tf_op jit(solution)/shard_map/triangular_solve/custom-call.0 | solution.py:13
  146.7 1.1 convolution_bitcast_fusion.1
  147.8 1.6 fusion.4
  149.5 70.5 %all-reduce.7.cloned.1.call-done = f32[2,448,32]{1,2,0:T(8,128)} async-done(((f32[2,448,32]{1,2,0:T(8,128)}), f32[2,448,32]{1,2,0:T(8,128)}) %all-reduce.7.cloned.1.call-update) | async-done | bytes 114704 | tf_op jit(solution)/shard_map/psum | solution.py:30
  220.0 2.3 fusion.2
  222.4 0.6 copy-done.8
  223.0 0.2 copy.31
  223.2 0.7 copy-done.5
  223.9 0.2 copy.32
  224.1 35.5 %psum.39 = f32[5,448]{1,0:T(8,128)S(1)} all-reduce(f32[5,448]{1,0:T(8,128)S(1)} %bitcast_convert_fusion), channel_id=1, replica_groups=mesh['dp'=8,'tensor'=4] {'dp'}, use_global_device_ids=true, to_apply=%region_6.9 | all-reduce | flops 2240 | bytes 17920 | tf_op jit(solution)/shard_map/psum | solution.py:49
  259.6 84.4 %all-reduce.9.cloned.1.call-done = f32[2,256,32]{1,2,0:T(8,128)} async-done(((f32[2,256,32]{1,2,0:T(8,128)}), f32[2,256,32]{1,2,0:T(8,128)}) %all-reduce.9.cloned.1.call-update) | async-done | bytes 65552 | tf_op jit(solution)/shard_map/psum | solution.py:20
  344.0 1.1 fusion.14
  345.2 5.9 %custom-call.10 = f32[2,32,32]{2,1,0:T(8,128)S(1)} custom-call(f32[2,32,32]{2,1,0:T(8,128)S(1)} %fusion.10), custom_call_target="Cholesky" | custom-call | tf_op jit(solution)/shard_map/jit(cholesky)/cholesky | solution.py:12
  351.3 4.9 %custom-call.11 = f32[2,1,32,32]{2,3,1,0:T(8,128)S(1)} custom-call(f32[2,1,32,32]{3,2,1,0:T(8,128)S(1)} %select_bitcast_fusion), custom_call_target="InvertDiagBlocksLowerTriangular" | custom-call | tf_op jit(solution)/shard_map/triangular_solve/custom-call.0 | solution.py:13
  356.2 0.3 convolution_bitcast_fusion
  356.5 1.6 fusion
  358.1 0.7 copy-done.6
  358.8 0.6 multiply_subtract_fusion
  359.4 69.2 %all-reduce.11.cloned.1.call-done = f32[2,448,32]{1,2,0:T(8,128)} async-done(((f32[2,448,32]{1,2,0:T(8,128)}), f32[2,448,32]{1,2,0:T(8,128)}) %all-reduce.11.cloned.1.call-update) | async-done | bytes 114704 | tf_op jit(solution)/shard_map/psum | solution.py:30
  428.7 1.8 convolution_multiply_fusion
  430.5 1.1 fusion.8
  431.6 0.2 subtract_convert_fusion
  431.8 0.1 copy.33
  431.9 0.8 copy.34
  432.8 31.5 %all_gather.3 = bf16[2,256,448]{2,0,1:T(2,128)(2,1)S(1)} all-gather(bf16[2,32,448]{2,0,1:T(2,128)(2,1)S(1)} %copy.33), channel_id=1, replica_groups=mesh['dp'=8,'tensor'=4] {'dp'}, dimensions={1}, use_global_device_ids=true | all-gather | bytes 516096 | tf_op jit(solution)/shard_map/all_gather | solution.py:40
  464.3 1.1 copy.35
  (34 shorter events, 0.8 us)
Async XLA Ops:
  7.2 0.9 copy-start
  7.2 140.6 %copy-start.1 = (f32[1,2,256,448]{2,3,1,0:T(8,128)S(1)}, f32[1,2,256,448]{2,3,1,0:T(8,128)}, u32[]{:S(2)}) copy-start(f32[1,2,256,448]{2,3,1,0:T(8,128)} %param.12) | copy-start | bytes 2752516
  7.2 127.3 %all-reduce.5.cloned.1.call-start = ((), (), s32[]{:S(2)}) async-start(), calls=%async_computation | async-start | bytes 131072 | tf_op jit(solution)/shard_map/psum | solution.py:20
  10.7 137.1 %copy-start.2 = (bf16[1,2,256,448]{2,3,1,0:T(8,128)(2,1)S(1)}, bf16[1,2,256,448]{2,3,1,0:T(8,128)(2,1)}, u32[]{:S(2)}) copy-start(bf16[1,2,256,448]{2,3,1,0:T(8,128)(2,1)} %param.11) | copy-start | bytes 1376260
  10.7 209.3 %all-reduce.7.cloned.1.call-start = ((), (), s32[]{:S(2)}) async-start(), calls=%async_computation.1 | async-start | bytes 262144 | tf_op jit(solution)/shard_map/psum | solution.py:30
  149.5 194.5 %all-reduce.9.cloned.1.call-start = ((), (), s32[]{:S(2)}) async-start(), calls=%async_computation.2 | async-start | bytes 131072 | tf_op jit(solution)/shard_map/psum | solution.py:20
  220.0 3.0 copy-start.4
  222.3 0.7 copy-start.8
  222.3 206.3 %all-reduce.11.cloned.1.call-start = ((), (), s32[]{:S(2)}) async-start(), calls=%async_computation.3 | async-start | bytes 262144 | tf_op jit(solution)/shard_map/psum | solution.py:30
  223.0 0.9 copy-start.5
  345.1 11.0 %copy-start.3 = (f32[2,256,32]{1,2,0:T(8,128)S(1)}, f32[2,256,32]{1,2,0:T(8,128)}, u32[]{:S(2)}) copy-start(f32[2,256,32]{1,2,0:T(8,128)} %all-reduce.9.cloned.1.call-done) | copy-start | bytes 196612
  358.1 0.7 copy-start.6
  358.1 0.7 copy-start.7
Sparse Core Ops, SparseCore 0:
  14.2 120.2 all-reduce.4
  149.6 70.3 all-reduce.6
  227.1 116.7 all-reduce.8
  358.2 70.3 all-reduce.10
where the time goes:
time: 472 us
  waiting for transfers between devices  348 us (74%)
  blocking collectives  67 us (14%)
  other arithmetic  23.9 us (5%)
  between operations  13.9 us (3%)
  matrix products  13.6 us (3%)
  local copies, waits for them, and re-layouts  5.47 us (1%)
    psum x2, waiting for transfers between devices, left_basis(): summed = lax.psum(partial_value, ('dp', 'tensor'))  208 us
    psum x2, waiting for transfers between devices, update(): right_f = lax.psum(right_part, 'dp')  140 us
    psum x1, blocking collectives, per_device(): vector_total = lax.psum(vector_grads[0].astype(jnp.float32), 'dp')  35.5 us
    all_gather x1, blocking collectives, update(): regathered = lax.all_gather(fresh_weights, 'dp', axis=1, tiled=True)  31.5 us
    another operation x7, other arithmetic, basis_from(): factor_low = jnp.linalg.cholesky(gram_mat)  12 us
    another operation x5, other arithmetic, basis_from(): lax.linalg.triangular_solve(factor_low, summed, left_side=False, lower=Tr...  9.99 us
  transfers between devices with their start and end apart: 4, of which 4 were waited for; matrix products, arithmetic and copies ran while one was open for 0% of the time, Pallas kernels for 0%

commit v1 on v0

--- a/solution.py
+++ b/solution.py
@@ -6,6 +6,27 @@
 ROUNDS = 2
 momentum_coef = 0.9
 step_rate = 0.1
+
+
+def laid_out(blocks, dim):
+    blocks = jnp.moveaxis(blocks, 0, dim)
+    lengths = blocks.shape
+    return blocks.reshape(*lengths[:dim], lengths[dim] * lengths[dim + 1], *lengths[dim + 2 :])
+
+
+def doubled(array, axis):
+    size, mine = (lax.axis_size(axis), lax.axis_index(axis))
+    blocks, bit = (array[None], 1)
+    while bit < size:
+        other = lax.ppermute(blocks, axis, [(i, i ^ bit) for i in range(size)])
+        low = mine & bit == 0
+        blocks = jnp.concatenate([jnp.where(low, blocks, other), jnp.where(low, other, blocks)])
+        bit *= 2
+    return blocks
+
+
+def gather_by_bits(x, axis, dim):
+    return laid_out(doubled(x, axis), dim)
 
 
 def basis_from(gram_mat, summed):
@@ -37,7 +58,7 @@
     my_rows = lax.dynamic_slice_in_dim(approx, lax.axis_index("dp") * own_rows, own_rows, 1)
     fresh_moments = momentum_coef * moments + my_rows
     fresh_weights = (weights - step_rate * fresh_moments).astype(jnp.bfloat16)
-    regathered = lax.all_gather(fresh_weights, "dp", axis=1, tiled=True)
+    regathered = gather_by_bits(fresh_weights, "dp", 1)
     return (fresh_errors, fresh_moments, regathered)
 
 

time: 472 us -> 493 us (1.044)
  waiting for transfers between devices: 348 us -> 395 us
  blocking collectives: 67 us -> 36 us
    psum x2, waiting for transfers between devices: 208 us -> 245 us  [left_basis(): summed = lax.psum(partial_value, ('dp', 'tensor'))]
    all_gather x1 -> x0, blocking collectives: 31.5 us -> none  [update(): regathered = lax.all_gather(fresh_weights, 'dp', axis=1, tiled=True)]
    ppermute x0 -> x3, waiting for transfers between devices: none -> 11.3 us  [doubled(): other = lax.ppermute(blocks, axis, [(i, i ^ bit) for i in range(size)])]
  transfers between devices with their start and end apart: 4 -> 7, of which waited for: 4 -> 6; matrix products, arithmetic and copies ran while one was open for 0% -> 1% of each run, Pallas kernels for 0% -> 0%
where the time goes in v1:
time: 493 us; the launch traced here: 492 us
  waiting for transfers between devices  395 us (80%)
  blocking collectives  36 us (7%)
  other arithmetic  25.9 us (5%)
  between operations  14 us (3%)
  matrix products  13.6 us (3%)
  local copies, waits for them, and re-layouts  6.46 us (1%)
    psum x2, waiting for transfers between devices, left_basis(): summed = lax.psum(partial_value, ('dp', 'tensor'))  245 us
    psum x2, waiting for transfers between devices, update(): right_f = lax.psum(right_part, 'dp')  138 us
    psum x1, blocking collectives, per_device(): vector_total = lax.psum(vector_grads[0].astype(jnp.float32), 'dp')  36 us
    another operation x7, other arithmetic, basis_from(): factor_low = jnp.linalg.cholesky(gram_mat)  12 us
    ppermute x3, waiting for transfers between devices, doubled(): other = lax.ppermute(blocks, axis, [(i, i ^ bit) for i in range(size)])  11.3 us
    another operation x5, other arithmetic, basis_from(): lax.linalg.triangular_solve(factor_low, summed, left_side=False, lower=Tr...  9.99 us
  transfers between devices with their start and end apart: 7, of which 6 were waited for; matrix products, arithmetic and copies ran while one was open for 1% of the time, Pallas kernels for 0%

profile of v1, /device:TPU:0, one launch (start us, length us, event | category | flops | bytes accessed | tf_op | source)
XLA Modules:
  0.0 492.1 jit_solution(14338834570174390373)
XLA Ops:
  7.2 0.8 copy-done
  8.1 2.6 fusion.6
  10.8 123.6 %all-reduce.5.cloned.1.call-done = f32[2,256,32]{1,2,0:T(8,128)} async-done(((f32[2,256,32]{1,2,0:T(8,128)}), f32[2,256,32]{1,2,0:T(8,128)}) %all-reduce.5.cloned.1.call-update) | async-done | bytes 65552 | tf_op jit(solution)/shard_map/psum | solution.py:41
  134.5 1.1 fusion.14
  135.6 5.9 %custom-call.8 = f32[2,32,32]{2,1,0:T(8,128)S(1)} custom-call(f32[2,32,32]{2,1,0:T(8,128)S(1)} %fusion.13), custom_call_target="Cholesky" | custom-call | tf_op jit(solution)/shard_map/jit(cholesky)/cholesky | solution.py:33
  141.7 4.9 custom-call.9
  146.7 1.1 convolution_bitcast_fusion.1
  147.8 1.6 fusion.4
  149.5 70.5 %all-reduce.7.cloned.1.call-done = f32[2,448,32]{1,2,0:T(8,128)} async-done(((f32[2,448,32]{1,2,0:T(8,128)}), f32[2,448,32]{1,2,0:T(8,128)}) %all-reduce.7.cloned.1.call-update) | async-done | bytes 114704 | tf_op jit(solution)/shard_map/psum | solution.py:51
  220.0 2.2 fusion.2
  222.4 121.6 %all-reduce.9.cloned.1.call-done = f32[2,256,32]{1,2,0:T(8,128)} async-done(((f32[2,256,32]{1,2,0:T(8,128)}), f32[2,256,32]{1,2,0:T(8,128)}) %all-reduce.9.cloned.1.call-update) | async-done | bytes 65552 | tf_op jit(solution)/shard_map/psum | solution.py:41
  344.0 1.1 fusion.15
  345.2 5.9 %custom-call.10 = f32[2,32,32]{2,1,0:T(8,128)S(1)} custom-call(f32[2,32,32]{2,1,0:T(8,128)S(1)} %fusion.11), custom_call_target="Cholesky" | custom-call | tf_op jit(solution)/shard_map/jit(cholesky)/cholesky | solution.py:33
  351.3 4.9 custom-call.11
  356.2 0.3 convolution_bitcast_fusion
  356.5 1.6 fusion
  358.1 0.9 copy-done.5
  359.2 0.7 copy-done.6
  359.9 1.0 copy.43
  360.9 67.8 %all-reduce.11.cloned.1.call-done = f32[2,448,32]{1,2,0:T(8,128)} async-done(((f32[2,448,32]{1,2,0:T(8,128)}), f32[2,448,32]{1,2,0:T(8,128)}) %all-reduce.11.cloned.1.call-update) | async-done | bytes 114704 | tf_op jit(solution)/shard_map/psum | solution.py:51
  428.7 1.9 convolution_multiply_fusion
  430.6 0.9 fusion.9
  431.5 0.8 collective-permute-start
  432.3 36.0 %psum.39 = f32[5,448]{1,0:T(8,128)S(1)} all-reduce(f32[5,448]{1,0:T(8,128)S(1)} %bitcast_convert_fusion), channel_id=1, replica_groups=mesh['dp'=8,'tensor'=4] {'dp'}, use_global_device_ids=true, to_apply=%region_6.9 | all-reduce | flops 2240 | bytes 17920 | tf_op jit(solution)/shard_map/psum | solution.py:70
  468.3 1.1 broadcast_select_fusion.3
  469.8 0.6 copy-done.7
  470.4 0.6 multiply_subtract_fusion
  471.0 0.8 copy.47
  471.8 2.9 collective-permute-done.1
  474.9 1.1 fusion.8
  475.9 8.4 %collective-permute-done.2 = bf16[4,2,32,448]{3,2,1,0:T(8,128)(2,1)S(1)} collective-permute-done((bf16[4,2,32,448]{3,2,1,0:T(8,128)(2,1)S(1)}, bf16[4,2,32,448]{3,2,1,0:T(8,128)(2,1)S(1)}, u32[]{:S(2)}, u32[]{:S(2)}) %collective-permute-start.2) | collective-permute-done | bytes 229408 | tf_op jit(solution)/shard_map/ppermute | solution.py:21
  484.5 1.0 copy.48
  (49 shorter events, 1.7 us)
Async XLA Ops:
  7.2 0.9 copy-start
  7.2 140.6 %copy-start.1 = (f32[1,2,256,448]{2,3,1,0:T(8,128)S(1)}, f32[1,2,256,448]{2,3,1,0:T(8,128)}, u32[]{:S(2)}) copy-start(f32[1,2,256,448]{2,3,1,0:T(8,128)} %param.12) | copy-start | bytes 2752516
  7.2 127.3 %all-reduce.5.cloned.1.call-start = ((), (), s32[]{:S(2)}) async-start(), calls=%async_computation | async-start | bytes 131072 | tf_op jit(solution)/shard_map/psum | solution.py:41
  10.7 137.1 %copy-start.2 = (bf16[1,2,256,448]{2,3,1,0:T(8,128)(2,1)S(1)}, bf16[1,2,256,448]{2,3,1,0:T(8,128)(2,1)}, u32[]{:S(2)}) copy-start(bf16[1,2,256,448]{2,3,1,0:T(8,128)(2,1)} %param.11) | copy-start | bytes 1376260
  10.7 209.3 %all-reduce.7.cloned.1.call-start = ((), (), s32[]{:S(2)}) async-start(), calls=%async_computation.1 | async-start | bytes 262144 | tf_op jit(solution)/shard_map/psum | solution.py:51
  149.5 194.5 %all-reduce.9.cloned.1.call-start = ((), (), s32[]{:S(2)}) async-start(), calls=%async_computation.2 | async-start | bytes 131072 | tf_op jit(solution)/shard_map/psum | solution.py:41
  222.3 206.4 %all-reduce.11.cloned.1.call-start = ((), (), s32[]{:S(2)}) async-start(), calls=%async_computation.3 | async-start | bytes 262144 | tf_op jit(solution)/shard_map/psum | solution.py:51
  345.2 11.0 %copy-start.4 = (f32[2,256,32]{1,2,0:T(8,128)S(1)}, f32[2,256,32]{1,2,0:T(8,128)}, u32[]{:S(2)}) copy-start(f32[2,256,32]{1,2,0:T(8,128)} %all-reduce.9.cloned.1.call-done) | copy-start | bytes 196612
  358.1 0.9 copy-start.5
  359.0 0.9 copy-start.6
  428.7 1.9 copy-start.3
  430.6 1.7 copy-start.9
  431.5 36.8 %collective-permute-start = (bf16[1,2,32,448]{2,3,1,0:T(8,128)(2,1)}, bf16[1,2,32,448]{2,3,1,0:T(8,128)(2,1)}, u32[]{:S(2)}, u32[]{:S(2)}) collective-permute-start(bf16[1,2,32,448]{2,3,1,0:T(8,128)(2,1)} %get-tuple-element.29), channel_id=1, source_target_pairs={{0,4},{4,0},{8,12},{12,8},{16,20},{20,16},{24,28},{28,24},{1,5},{5... | collective-permute-start | bytes 172040 | tf_op jit(solution)/shard_map/ppermute | solution.py:21
  469.6 0.7 copy-start.7
  469.6 0.7 copy-start.8
  469.7 5.0 %collective-permute-start.1 = (bf16[2,2,32,448]{3,2,1,0:T(8,128)(2,1)S(1)}, bf16[2,2,32,448]{3,2,1,0:T(8,128)(2,1)S(1)}, u32[]{:S(2)}, u32[]{:S(2)}) collective-permute-start(bf16[2,2,32,448]{3,2,1,0:T(8,128)(2,1)S(1)} %pad_maximum_fusion.1), channel_id=1, source_target_pairs={{0,8},{4,12},{8,0},{12,4},{16,24},{20,28},{24,16},{28,20},{1,9},{5... | collective-permute-start | bytes 344072 | tf_op jit(solution)/shard_map/ppermute | solution.py:21
  474.8 9.6 %collective-permute-start.2 = (bf16[4,2,32,448]{3,2,1,0:T(8,128)(2,1)S(1)}, bf16[4,2,32,448]{3,2,1,0:T(8,128)(2,1)S(1)}, u32[]{:S(2)}, u32[]{:S(2)}) collective-permute-start(bf16[4,2,32,448]{3,2,1,0:T(8,128)(2,1)S(1)} %pad_maximum_fusion), channel_id=1, source_target_pairs={{0,16},{4,20},{8,24},{12,28},{16,0},{20,4},{24,8},{28,12},{1,17},{... | collective-permute-start | bytes 688136 | tf_op jit(solution)/shard_map/ppermute | solution.py:21
Sparse Core Ops, SparseCore 0:
  14.2 120.2 all-reduce.4
  149.6 70.4 all-reduce.6
  227.1 116.7 all-reduce.8
  358.2 70.4 all-reduce.10
